TPU v7x, 128 devices: a whole 4x4x4 slice. The times are simulated.
128 devices in a mesh: row: 8 (over z_hi, x), blk: 16 (over z_lo, y, core).
Axes of the slice: x: 4, y: 4, z: 4 (z_hi: 2, z_lo: 2; z = z_hi * 2 + z_lo), core: 2. Of those that a mesh axis runs over, the one named last changes fastest.
Arguments:
- spike_counts: int32 [16384, 2048], P(('row', 'blk')), may hold values from 0 to 23, as said below
- kernel_taps: int32 [16], replicated, may hold values from 1 to 8
- lag_bins: int32 [2], replicated, may hold values from 1 to 32, as said below
Outputs:
- correlogram: bfloat16 [2, 16384, 8, 2048], P(None, 'row', None, 'blk')
Inputs may be any that keep to these rules, and one draw needn't show every extreme that they name: `spike_counts`: neurons fire at different rates and share a common drive. `lag_bins`: the second lag equals 32; the first lies between 1 and 31.
All inputs are finite; a program needn't handle non-finite values.
Results may differ from a plain program's by a relative error of at most 0.0034.
Values may be sent and summed in bfloat16 or wider, within the bound.
A program may use at most 128 MiB of HBM per device.

v0:
```python
import jax
import jax.numpy as jnp
from jax import lax
from jax.sharding import PartitionSpec as P

NEURONS = 16384
BINS = 2048
TAPS = 16


def smoothed(spike_counts, kernel_taps):
    counts = spike_counts.astype(jnp.float32)
    weights = kernel_taps.astype(jnp.float32) / jnp.sum(kernel_taps.astype(jnp.float32))
    padded = jnp.pad(counts, ((0, 0), (TAPS - 1, 0)))
    result = jnp.zeros_like(counts)
    for delay in range(TAPS):
        result = result + weights[delay] * padded[:, TAPS - 1 - delay : TAPS - 1 - delay + BINS]
    return result


def later_bins(data, lag):
    padded = jnp.pad(data, ((0, 0), (0, BINS)))
    return lax.dynamic_slice_in_dim(padded, lag, BINS, 1)


def shards(spike_counts, kernel_taps, lag_bins):
    smooth = smoothed(spike_counts, kernel_taps)
    centred = smooth - jnp.mean(smooth, axis=1, keepdims=True)
    totals = lax.psum(jnp.sum(centred, axis=0), ("row", "blk"))
    residual_part = centred - (totals / NEURONS)[None, :]
    zscored = (
        residual_part
        * lax.rsqrt(jnp.mean(residual_part * residual_part, axis=1, keepdims=True) + 1e-05)
    ).astype(jnp.bfloat16)
    span_rows = zscored.shape[0]
    groups = lax.axis_size("row")
    columns = lax.all_gather(zscored, "row", axis=0, tiled=True)
    stacked = jnp.concatenate(
        [later_bins(columns, lag_bins[0]), later_bins(columns, lag_bins[1])], axis=0
    )
    piece = lax.all_gather(zscored, "blk", axis=0, tiled=True)
    product = jnp.dot(piece, stacked.T, preferred_element_type=jnp.float32) / BINS
    product = product.reshape(piece.shape[0], 2, groups, span_rows)
    return jnp.transpose(product, (1, 0, 2, 3)).astype(jnp.bfloat16)


def solution(mesh):
    placed = (P(("row", "blk"), None), P(), P())
    return jax.shard_map(
        shards, mesh=mesh, in_specs=placed, out_specs=P(None, "row", None, "blk"), check_vma=False
    )
```

profile of v0, /device:TPU:1, one launch (start us, length us, event | category | flops | bytes accessed | tf_op | source)
XLA Modules:
  0.0 258.9 jit_solution(15566849793997691235)
XLA Ops:
  6.5 0.0 copy-start
  6.5 0.0 all-gather.5.cloned.1.call-start
  6.5 1.3 convert_reduce_fusion
  7.8 1.3 convert_divide_fusion
  9.1 0.7 fusion.8
  9.8 1.3 convert_element_type.25
  11.2 14.1 %fusion.6 = (f32[128]{0:T(128)S(1)}, f32[128,2048]{1,0:T(8,128)S(1)}) fusion(f32[]{:T(128)} %bitcast.15, f32[]{:T(128)} %bitcast.14, f32[]{:T(128)} %bitcast.13, f32[]{:T(128)} %bitcast.12, f32[]{:T(128)} %bitcast.11, f32[]{:T(128)} %bitcast.10, f32[]{:T(128)} %bitcast.9, f32[]{:T(128)} %bitcast.8, f32[]{:T(128)} %bitcast.7, f32[]{:T(128)} %bitcast.6, ...), kind=kLoop, calls=%fused_computation.19 | loop fusion | flops 8388480 | bytes 2097728 | tf_op jit(solution)/shard_map/reduce_sum | solution.py:28
  25.3 0.2 subtract_reduce_fusion
  25.5 68.7 %psum.7 = f32[2048]{0:T(1024)S(1)} all-reduce(f32[2048]{0:T(1024)S(1)} %subtract_reduce_fusion), channel_id=1, replica_groups=mesh['row'=8,'blk'=16] {'row','blk'}, use_global_device_ids=true, to_apply=%region_3.4 | all-reduce | flops 2048 | bytes 16384 | tf_op jit(solution)/shard_map/psum | solution.py:29
  94.2 0.3 multiply_reduce_fusion
  94.5 1.0 multiply_convert_fusion.1
  95.5 0.0 all-gather.5.cloned.1.call-update
  95.6 0.2 all-gather.3.cloned.1.call-start
  95.8 0.5 all-gather.3.cloned.1.call-update
  96.3 0.0 copy-done
  96.3 0.6 fusion.7
  100.7 62.5 %all-gather.5.cloned.1.call-done = bf16[1024,2048]{1,0:T(8,128)(2,1)} async-done(((bf16[128,2048]{1,0:T(8,128)(2,1)}), bf16[1024,2048]{1,0:T(8,128)(2,1)}) %all-gather.5.cloned.1.call-update) | async-done | bytes 4194320 | tf_op jit(solution)/shard_map/all_gather | solution.py:37
  163.2 10.0 %pad_dynamic-slice_fusion.1 = (bf16[1024,2048]{1,0:T(8,128)(2,1)}, bf16[1024,2048]{1,0:T(8,128)(2,1)}) fusion(s32[]{:T(128)S(6)} %select_n.6, bf16[1024,2048]{1,0:T(8,128)(2,1)} %all-gather.5.cloned.1.call-done, s32[]{:T(128)S(6)} %select_n.7), kind=kLoop, calls=%fused_computation.2 | loop fusion | bytes 12582920 | tf_op jit(solution)/shard_map/dynamic_slice | solution.py:23
  173.2 42.5 %all-gather.3.cloned.1.call-done = bf16[2048,2048]{1,0:T(8,128)(2,1)} async-done(((bf16[128,2048]{1,0:T(8,128)(2,1)}), bf16[2048,2048]{1,0:T(8,128)(2,1)}) %all-gather.3.cloned.1.call-update) | async-done | bytes 8388624 | tf_op jit(solution)/shard_map/all_gather | solution.py:41
  215.7 23.8 %multiply_convert_fusion = bf16[2048,2048]{0,1:T(8,128)(2,1)} fusion(bf16[2048,2048]{1,0:T(8,128)(2,1)} %all-gather.3.cloned.1.call-done, bf16[1024,2048]{1,0:T(8,128)(2,1)} %get-tuple-element.8, bf16[1024,2048]{1,0:T(8,128)(2,1)} %get-tuple-element.7), kind=kOutput, calls=%fused_computation | convolution fusion | flops 17205035008 | bytes 25165824 | tf_op jit(solution)/shard_map/dot_general | solution.py:42
  239.5 12.6 %copy.4 = bf16[2048,2,8,128]{3,2,0,1:T(8,128)(2,1)} copy(bf16[2048,2,8,128]{0,3,2,1:T(8,128)(2,1)} %bitcast.21) | data formatting | bytes 16777216 | tf_op jit(solution)/shard_map/convert_element_type | solution.py:44
  (3 shorter events, 0.0 us)
Async XLA Ops:
  6.5 89.8 %copy-start = (s32[2]{0:T(128)S(1)}, s32[2]{0:T(128)}, u32[]{:S(2)}) copy-start(s32[2]{0:T(128)} %param.5) | copy-start | bytes 28
  6.5 156.7 %all-gather.5.cloned.1.call-start = ((), (), s32[]{:S(2)}) async-start(), calls=%async_computation.1 | async-start | bytes 4718592 | tf_op jit(solution)/shard_map/all_gather | solution.py:37
  95.6 120.2 %all-gather.3.cloned.1.call-start = ((), (), s32[]{:S(2)}) async-start(), calls=%async_computation | async-start | bytes 8912896 | tf_op jit(solution)/shard_map/all_gather | solution.py:41
Sparse Core Ops, SparseCore 0:
  95.7 67.5 all-gather.4
  165.0 50.7 all-gather.2
where the time goes:
time: 260 us; the launch traced here: 259 us
  waiting for transfers between devices  106 us (41%)
  blocking collectives  68.7 us (26%)
  local copies, waits for them, and re-layouts  23.9 us (9%)
  matrix products  23.8 us (9%)
  other arithmetic  19.5 us (8%)
  between operations  17.2 us (7%)
    psum x1, blocking collectives, shards(): totals = lax.psum(jnp.sum(centred, axis=0), ('row', 'blk'))  68.7 us
    all_gather x1, waiting for transfers between devices, shards(): columns = lax.all_gather(zscored, 'row', axis=0, tiled=True)  62.5 us
    all_gather x1, waiting for transfers between devices, shards(): piece = lax.all_gather(zscored, 'blk', axis=0, tiled=True)  42.5 us
    dot_general x1, matrix products, shards(): jnp.dot(piece, stacked.T, preferred_element_type=jnp.float32) / BINS  23.8 us
    reduce_sum x1, other arithmetic, shards(): centred = smooth - jnp.mean(smooth, axis=1, keepdims=True)  14.1 us
    convert_element_type x1, local copies, waits for them, and re-layouts, shards(): return jnp.transpose(product, (1, 0, 2, 3)).astype(jnp.bfloat16)  12.6 us
    dynamic_slice x1, local copies, waits for them, and re-layouts, later_bins(): return lax.dynamic_slice_in_dim(padded, lag, BINS, 1)  9.97 us
  transfers between devices with their start and end apart: 2, of which 2 were waited for; matrix products, arithmetic and copies ran while one was open for 4% of the time, Pallas kernels for 0%

commit v1 on v0

--- a/solution.py
+++ b/solution.py
@@ -26,7 +26,9 @@
 def shards(spike_counts, kernel_taps, lag_bins):
     smooth = smoothed(spike_counts, kernel_taps)
     centred = smooth - jnp.mean(smooth, axis=1, keepdims=True)
-    totals = lax.psum(jnp.sum(centred, axis=0), ("row", "blk"))
+    x = jnp.sum(centred, axis=0)
+    blocks = lax.all_gather(x, ("row", "blk"))
+    totals = jnp.sum(blocks, axis=0)
     residual_part = centred - (totals / NEURONS)[None, :]
     zscored = (
         residual_part

time: 260 us -> 389 us (1.50)
  waiting for transfers between devices: 106 us -> 302 us
  blocking collectives: 68.7 us -> 0 us
    all_gather x0 -> x1, waiting for transfers between devices: none -> 194 us  [shards(): blocks = lax.all_gather(x, ('row', 'blk'))]
    psum x1 -> x0, blocking collectives: 68.7 us -> none  [shards(): totals = lax.psum(jnp.sum(centred, axis=0), ('row', 'blk'))]
  transfers between devices with their start and end apart: 2 -> 3, of which waited for: 2 -> 3; matrix products, arithmetic and copies ran while one was open for 4% -> 3% of each run, Pallas kernels for 0% -> 0%
where the time goes in v1:
time: 389 us; the launch traced here: 388 us
  waiting for transfers between devices  302 us (78%)
  local copies, waits for them, and re-layouts  25.2 us (6%)
  matrix products  23.8 us (6%)
  other arithmetic  20.2 us (5%)
  between operations  16.9 us (4%)
    all_gather x1, waiting for transfers between devices, shards(): blocks = lax.all_gather(x, ('row', 'blk'))  194 us
    all_gather x1, waiting for transfers between devices, shards(): columns = lax.all_gather(zscored, 'row', axis=0, tiled=True)  65 us
    all_gather x1, waiting for transfers between devices, shards(): piece = lax.all_gather(zscored, 'blk', axis=0, tiled=True)  42.5 us
    dot_general x1, matrix products, shards(): jnp.dot(piece, stacked.T, preferred_element_type=jnp.float32) / BINS  23.8 us
    reduce_sum x1, other arithmetic, shards(): centred = smooth - jnp.mean(smooth, axis=1, keepdims=True)  14.1 us
    convert_element_type x1, local copies, waits for them, and re-layouts, shards(): return jnp.transpose(product, (1, 0, 2, 3)).astype(jnp.bfloat16)  12.6 us
    dynamic_slice x1, local copies, waits for them, and re-layouts, later_bins(): return lax.dynamic_slice_in_dim(padded, lag, BINS, 1)  9.97 us
  transfers between devices with their start and end apart: 3, of which 3 were waited for; matrix products, arithmetic and copies ran while one was open for 3% of the time, Pallas kernels for 0%

profile of v1, /device:TPU:1, one launch (start us, length us, event | category | flops | bytes accessed | tf_op | source)
XLA Modules:
  0.0 388.0 jit_solution(17461498117312077280)
XLA Ops:
  6.5 0.0 all-gather.9.cloned.1.call-start
  6.5 1.3 convert_reduce_fusion
  7.8 1.3 convert_divide_fusion
  9.1 0.7 fusion.8
  9.8 1.3 convert_element_type.25
  11.2 14.1 %fusion.6 = (f32[128]{0:T(128)S(1)}, f32[128,2048]{1,0:T(8,128)S(1)}) fusion(f32[]{:T(128)} %bitcast.15, f32[]{:T(128)} %bitcast.14, f32[]{:T(128)} %bitcast.13, f32[]{:T(128)} %bitcast.12, f32[]{:T(128)} %bitcast.11, f32[]{:T(128)} %bitcast.10, f32[]{:T(128)} %bitcast.9, f32[]{:T(128)} %bitcast.8, f32[]{:T(128)} %bitcast.7, f32[]{:T(128)} %bitcast.6, ...), kind=kLoop, calls=%fused_computation.19 | loop fusion | flops 8388480 | bytes 2097728 | tf_op jit(solution)/shard_map/reduce_sum | solution.py:28
  25.3 0.8 subtract_reduce_fusion
  26.1 0.0 all-gather.9.cloned.1.call-update
  26.1 0.0 all-gather.7.cloned.1.call-start
  26.1 193.7 %all-gather.9.cloned.1.call-done = f32[262144]{0:T(1024)} async-done(((f32[2048]{0:T(1024)}), f32[262144]{0:T(1024)}) %all-gather.9.cloned.1.call-update) | async-done | bytes 1048592 | tf_op jit(solution)/shard_map/all_gather | solution.py:30
  219.8 1.4 reshape.17
  221.2 0.1 reduce_sum.48
  221.3 0.3 multiply_reduce_fusion
  221.6 1.0 multiply_convert_fusion.1
  222.6 0.0 all-gather.7.cloned.1.call-update
  222.6 0.2 all-gather.5.cloned.1.call-start
  222.8 0.5 all-gather.5.cloned.1.call-update
  223.4 0.0 copy-done
  223.4 0.6 fusion.7
  227.8 65.0 %all-gather.7.cloned.1.call-done = bf16[1024,2048]{1,0:T(8,128)(2,1)} async-done(((bf16[128,2048]{1,0:T(8,128)(2,1)}), bf16[1024,2048]{1,0:T(8,128)(2,1)}) %all-gather.7.cloned.1.call-update) | async-done | bytes 4194320 | tf_op jit(solution)/shard_map/all_gather | solution.py:39
  292.7 10.0 %pad_dynamic-slice_fusion.1 = (bf16[1024,2048]{1,0:T(8,128)(2,1)}, bf16[1024,2048]{1,0:T(8,128)(2,1)}) fusion(s32[]{:T(128)S(6)} %select_n.6, bf16[1024,2048]{1,0:T(8,128)(2,1)} %all-gather.7.cloned.1.call-done, s32[]{:T(128)S(6)} %select_n.7), kind=kLoop, calls=%fused_computation.2 | loop fusion | bytes 12582920 | tf_op jit(solution)/shard_map/dynamic_slice | solution.py:23
  302.7 42.5 %all-gather.5.cloned.1.call-done = bf16[2048,2048]{1,0:T(8,128)(2,1)} async-done(((bf16[128,2048]{1,0:T(8,128)(2,1)}), bf16[2048,2048]{1,0:T(8,128)(2,1)}) %all-gather.5.cloned.1.call-update) | async-done | bytes 8388624 | tf_op jit(solution)/shard_map/all_gather | solution.py:43
  345.2 23.8 %multiply_convert_fusion = bf16[2048,2048]{0,1:T(8,128)(2,1)} fusion(bf16[2048,2048]{1,0:T(8,128)(2,1)} %all-gather.5.cloned.1.call-done, bf16[1024,2048]{1,0:T(8,128)(2,1)} %get-tuple-element.8, bf16[1024,2048]{1,0:T(8,128)(2,1)} %get-tuple-element.7), kind=kOutput, calls=%fused_computation | convolution fusion | flops 17205035008 | bytes 25165824 | tf_op jit(solution)/shard_map/dot_general | solution.py:44
  369.0 12.6 %copy.6 = bf16[2048,2,8,128]{3,2,0,1:T(8,128)(2,1)} copy(bf16[2048,2,8,128]{0,3,2,1:T(8,128)(2,1)} %bitcast.21) | data formatting | bytes 16777216 | tf_op jit(solution)/shard_map/convert_element_type | solution.py:46
  (4 shorter events, 0.0 us)
Async XLA Ops:
  6.5 216.8 %copy-start = (s32[2]{0:T(128)S(1)}, s32[2]{0:T(128)}, u32[]{:S(2)}) copy-start(s32[2]{0:T(128)} %param.5) | copy-start | bytes 28
  6.5 213.3 %all-gather.9.cloned.1.call-start = ((), (), s32[]{:S(2)}) async-start(), calls=%async_computation.2 | async-start | bytes 1056768 | tf_op jit(solution)/shard_map/all_gather | solution.py:30
  26.1 266.7 %all-gather.7.cloned.1.call-start = ((), (), s32[]{:S(2)}) async-start(), calls=%async_computation.1 | async-start | bytes 4718592 | tf_op jit(solution)/shard_map/all_gather | solution.py:39
  222.6 122.6 %all-gather.5.cloned.1.call-start = ((), (), s32[]{:S(2)}) async-start(), calls=%async_computation | async-start | bytes 8912896 | tf_op jit(solution)/shard_map/all_gather | solution.py:43
Sparse Core Ops, SparseCore 0:
  26.2 193.5 all-gather.8
  222.7 69.9 all-gather.6
  294.4 50.7 all-gather.4
